TPU v7x, 32 devices: a whole 2x2x4 slice. The times are simulated.
32 devices in a mesh: sector: 4 (over y, x), term: 8 (over z, core).
Axes of the slice: x: 2, y: 2, z: 4, core: 2. Of those that a mesh axis runs over, the one named last changes fastest.
Arguments:
- wavefunction: float32 [4, 256, 256], P('sector'), may hold values from -6 to 6
- left_env: float32 [384, 256, 256], P(('sector', 'term')), may hold values from -0.0390625 to 0.0390625
- right_env: float32 [384, 256, 256], P(('sector', 'term')), may hold values from -0.375 to 0.375
- in_sector: int32 [384], P(('sector', 'term')), may hold values from 0 to 3
- out_sector: int32 [384], P(('sector', 'term')), may hold values from 0 to 3
- precond: float32 [4, 256, 256], P('sector'), may hold values from 2 to 4
- shifts: float32 [2], replicated, may hold values from 0.2 to 1
Outputs:
- corrected: float32 [4, 256, 256], P('sector')
- residual_norms: float32 [2], replicated
All inputs are finite; a program needn't handle non-finite values.
Results may differ from a plain program's by a relative error of at most 0.0001.
Values sent between devices are 32-bit elements; how exact they have to be, the bound alone decides.
A program may use at most 64 MiB of HBM per device.

v0:
```python
import jax
import jax.numpy as jnp
from jax import lax
from jax.sharding import PartitionSpec as P

ITERS = 2


def apply_tasks(full, left_env, right_env, in_sector, out_sector):

    def one_task(total, item):
        left, right, source, target = item
        block = lax.dynamic_index_in_dim(full, source, 0, keepdims=False)
        middle = jnp.dot(
            left, block, precision=lax.Precision.HIGHEST, preferred_element_type=jnp.float32
        )
        result = jnp.dot(
            middle, right, precision=lax.Precision.HIGHEST, preferred_element_type=jnp.float32
        )
        current = lax.dynamic_index_in_dim(total, target, 0, keepdims=False)
        total = lax.dynamic_update_index_in_dim(total, current + result, target, 0)
        return (total, None)

    start = jnp.zeros(full.shape, jnp.float32)
    total, _ = lax.scan(one_task, start, (left_env, right_env, in_sector, out_sector))
    return total


def correction(sigma, psi, precond, shift):
    residual = sigma - shift * psi
    updated = psi - residual / (precond - shift)
    return (updated, jnp.sum(residual * residual), jnp.sum(updated * updated))


def per_device(wavefunction, left_env, right_env, in_sector, out_sector, precond, shifts):
    full = lax.all_gather(wavefunction, "sector", axis=0, tiled=True)
    norms = []
    psi = wavefunction
    count = lax.axis_size("sector") * psi.size
    for step in range(ITERS):
        partial_value = apply_tasks(full, left_env, right_env, in_sector, out_sector)
        owned = lax.psum_scatter(partial_value, "sector", scatter_dimension=0, tiled=True)
        sigma = lax.psum(owned, "term")
        updated, res_sq, upd_sq = correction(sigma, psi, precond, shifts[step])
        res_total, upd_total = lax.psum((res_sq, upd_sq), "sector")
        norms.append(jnp.sqrt(res_total))
        psi = updated / jnp.sqrt(upd_total / count + 1e-06)
        if step + 1 < ITERS:
            full = lax.all_gather(psi, "sector", axis=0, tiled=True)
    return (psi, jnp.stack(norms))


def solution(mesh):
    placed = (
        P("sector", None, None),
        P(("sector", "term"), None, None),
        P(("sector", "term"), None, None),
        P(("sector", "term")),
        P(("sector", "term")),
        P("sector", None, None),
        P(),
    )
    return jax.shard_map(
        per_device,
        mesh=mesh,
        in_specs=placed,
        out_specs=(P("sector", None, None), P()),
        check_vma=False,
    )
```

profile of v0, /device:TPU:0, one launch (start us, length us, event | category | flops | bytes accessed | tf_op | source)
XLA Modules:
  0.0 478.9 jit_solution(9953802204697645868)
XLA Ops:
  7.9 31.1 %all-gather.3.cloned.1.call-done = f32[4,256,256]{2,1,0:T(8,128)} async-done(((f32[1,256,256]{2,1,0:T(8,128)}), f32[4,256,256]{2,1,0:T(8,128)}) %all-gather.3.cloned.1.call-update) | async-done | bytes 1048592 | tf_op jit(solution)/shard_map/all_gather | solution.py:36
  39.2 110.3 %while.20 = (s32[]{:T(128)}, f32[4,256,256]{2,1,0:T(8,128)S(1)}, s32[12]{0:T(128)}, f32[12,256,256]{2,1,0:T(8,128)}, s32[12]{0:T(128)}, /*index=5*/f32[4,256,256...) while((s32[]{:T(128)}, f32[4,256,256]{2,1,0:T(8,128)S(1)}, s32[12]{0:T(128)}, ...), condition=%wide.region_1.2_spmd, body=%wide.region_0.1_spmd.sunk | while | flops 402718720 | bytes 2360525 | solution.py:25
  60.8 1.4 fusion.41
  79.2 1.4 fusion.41
  97.6 1.4 fusion.41
  116.0 1.4 fusion.41
  134.4 1.4 fusion.41
  150.6 28.0 %reduce-scatter.7.cloned.1.call-done = f32[1,256,256]{2,1,0:T(8,128)} async-done(((f32[4,256,256]{2,1,0:T(8,128)}), f32[1,256,256]{2,1,0:T(8,128)}) %reduce-scatter.7.cloned.1.call-update) | async-done | bytes 262160
  179.3 57.1 %all-reduce.6.cloned.1.call-done = f32[1,256,256]{2,1,0:T(8,128)} async-done(((f32[1,256,256]{2,1,0:T(8,128)}), f32[1,256,256]{2,1,0:T(8,128)}) %all-reduce.6.cloned.1.call-update) | async-done | bytes 262160 | tf_op jit(solution)/shard_map/psum | solution.py:43
  236.4 2.4 multiply_reduce_fusion.3
  238.8 10.4 %psum.43 = f32[]{:T(128)} all-reduce(f32[]{:T(128)} %get-tuple-element.111), channel_id=1, replica_groups=mesh['sector'=4,'term'=8] {'sector'}, use_global_device_ids=true, to_apply=%region_5.6 | all-reduce | flops 1 | bytes 8 | tf_op jit(solution)/shard_map/psum | solution.py:45
  250.7 23.8 %all-gather.5.cloned.1.call-done = f32[4,256,256]{2,1,0:T(8,128)} async-done(((f32[1,256,256]{2,1,0:T(8,128)}), f32[4,256,256]{2,1,0:T(8,128)}) %all-gather.5.cloned.1.call-update) | async-done | bytes 1048592 | tf_op jit(solution)/shard_map/all_gather | solution.py:49
  274.7 94.6 %while.21 = (s32[]{:T(128)}, f32[4,256,256]{2,1,0:T(8,128)S(1)}, s32[12]{0:T(128)S(1)}, f32[12,256,256]{2,1,0:T(8,128)}, s32[12]{0:T(128)S(1)}, /*index=5*/f32[4...) while((s32[]{:T(128)}, f32[4,256,256]{2,1,0:T(8,128)S(1)}, ...), condition=%wide.region_7.8_spmd, body=%wide.region_6.7_spmd.sunk | while | flops 402718720 | bytes 2360525 | solution.py:25
  285.1 1.4 fusion.47
  293.0 1.4 fusion.47
  300.8 1.4 fusion.47
  308.7 1.4 fusion.47
  316.6 1.4 fusion.47
  324.5 1.4 fusion.47
  332.4 1.4 fusion.47
  370.3 28.0 %reduce-scatter.9.cloned.1.call-done = f32[1,256,256]{2,1,0:T(8,128)} async-done(((f32[4,256,256]{2,1,0:T(8,128)}), f32[1,256,256]{2,1,0:T(8,128)}) %reduce-scatter.9.cloned.1.call-update) | async-done | bytes 262160
  398.4 57.6 %all-reduce.8.cloned.1.call-done = f32[1,256,256]{2,1,0:T(8,128)} async-done(((f32[1,256,256]{2,1,0:T(8,128)}), f32[1,256,256]{2,1,0:T(8,128)}) %all-reduce.8.cloned.1.call-update) | async-done | bytes 262160 | tf_op jit(solution)/shard_map/psum | solution.py:43
  455.9 2.2 multiply_reduce_fusion.2
  458.2 10.5 %all-reduce.2 = (f32[]{:T(128)}, f32[]{:T(128)}, f32[]{:T(128)}) all-reduce(f32[]{:T(128)} %get-tuple-element.109, f32[]{:T(128)} %get-tuple-element.114, f32[]{:T(128)} %get-tuple-element.113), channel_id=1, replica_groups=mesh['sector'=4,'term'=8] {'sector'}, use_global_device_ids=true, to_apply=%region_11.12 | all-reduce | flops 3 | bytes 24 | tf_op jit(solution)/shard_map/psum | solution.py:45
  (140 shorter events, 99.4 us)
Async XLA Ops:
  7.2 31.9 %all-gather.3.cloned.1.call-start = ((), (), s32[]{:S(2)}) async-start(), calls=%async_computation.2 | async-start | bytes 1310720 | tf_op jit(solution)/shard_map/all_gather | solution.py:36
  7.9 170.7 %reduce-scatter.7.cloned.1.call-start = ((), (), s32[]{:S(2)}) async-start(), calls=%async_computation.6 | async-start | bytes 1310720
  39.2 139.6 %copy-start.4 = (f32[2]{0:T(128)S(1)}, f32[2]{0:T(128)}, u32[]{:S(2)}) copy-start(f32[2]{0:T(128)} %param.17) | copy-start | bytes 28
  39.2 197.2 %copy-start.2 = (f32[1,256,256]{2,1,0:T(8,128)S(1)}, f32[1,256,256]{2,1,0:T(8,128)}, u32[]{:S(2)}) copy-start(f32[1,256,256]{2,1,0:T(8,128)} %param.11) | copy-start | bytes 786436
  39.2 197.2 %copy-start.3 = (f32[1,256,256]{2,1,0:T(8,128)S(1)}, f32[1,256,256]{2,1,0:T(8,128)}, u32[]{:S(2)}) copy-start(f32[1,256,256]{2,1,0:T(8,128)} %param.16) | copy-start | bytes 786436
  149.5 1.0 copy-start.1
  149.6 125.1 %copy-start.5 = (s32[12]{0:T(128)S(1)}, s32[12]{0:T(128)}, u32[]{:S(2)}) copy-start(s32[12]{0:T(128)} %get-tuple-element.289) | copy-start | bytes 148
  149.6 125.1 %copy-start.6 = (s32[12]{0:T(128)S(1)}, s32[12]{0:T(128)}, u32[]{:S(2)}) copy-start(s32[12]{0:T(128)} %get-tuple-element.290) | copy-start | bytes 148
  150.5 85.9 %all-reduce.6.cloned.1.call-start = ((), (), s32[]{:S(2)}) async-start(), calls=%async_computation.3 | async-start | bytes 524288 | tf_op jit(solution)/shard_map/psum | solution.py:43
  178.7 95.9 %all-gather.5.cloned.1.call-start = ((), (), s32[]{:S(2)}) async-start(), calls=%async_computation.4 | async-start | bytes 1310720 | tf_op jit(solution)/shard_map/all_gather | solution.py:49
  250.7 147.7 %reduce-scatter.9.cloned.1.call-start = ((), (), s32[]{:S(2)}) async-start(), calls=%async_computation.7 | async-start | bytes 1310720
  369.2 1.0 copy-start
  370.2 85.7 %all-reduce.8.cloned.1.call-start = ((), (), s32[]{:S(2)}) async-start(), calls=%async_computation.5 | async-start | bytes 524288 | tf_op jit(solution)/shard_map/psum | solution.py:43
Sparse Core Ops, SparseCore 0:
  9.8 29.2 all-gather.2
  150.7 27.9 reduce-scatter.6
  181.0 55.4 all-reduce.5
  250.8 23.7 all-gather.4
  370.4 27.9 reduce-scatter.8
  400.5 55.4 all-reduce.7
where the time goes:
time: 482 us; the launch traced here: 479 us
  waiting for transfers between devices  226 us (47%)
  loops' own time  94.2 us (20%)
  matrix products  66.1 us (14%)
  local copies, waits for them, and re-layouts  47.3 us (10%)
  blocking collectives  20.9 us (4%)
  between operations  17 us (4%)
  other arithmetic  6.63 us (1%)
    psum x2, waiting for transfers between devices, per_device(): sigma = lax.psum(owned, 'term')  115 us
    another operation x2, loops' own time, apply_tasks(): lax.scan(one_task, start, (left_env, right_env, in_sector, out_sector))  94.2 us
    unnamed x8, waiting for transfers between devices  56.8 us
    dynamic_slice x48, local copies, waits for them, and re-layouts, apply_tasks(): lax.scan(one_task, start, (left_env, right_env, in_sector, out_sector))  44 us
    dot_general x24, matrix products, one_task(): jnp.dot(left, block, precision=lax.Precision.HIGHEST, preferred_element_t...  33.9 us
    dot_general x24, matrix products, one_task(): jnp.dot(middle, right, precision=lax.Precision.HIGHEST, preferred_element...  32.1 us
    all_gather x1, waiting for transfers between devices, per_device(): full = lax.all_gather(wavefunction, 'sector', axis=0, tiled=True)  31.1 us
    all_gather x1, waiting for transfers between devices, per_device(): full = lax.all_gather(psi, 'sector', axis=0, tiled=True)  23.8 us
  transfers between devices with their start and end apart: 6, of which 6 were waited for; matrix products, arithmetic and copies ran while one was open for 0% of the time, Pallas kernels for 0%

commit v1 on v0

--- a/solution.py
+++ b/solution.py
@@ -33,7 +33,14 @@
 
 
 def per_device(wavefunction, left_env, right_env, in_sector, out_sector, precond, shifts):
-    full = lax.all_gather(wavefunction, "sector", axis=0, tiled=True)
+    ring = [wavefunction]
+    for hop in range(3):
+        ring.append(lax.ppermute(ring[-1], "sector", [(dev, (dev + 1) % 4) for dev in range(4)]))
+    full = jnp.roll(
+        jnp.concatenate(ring[::-1], axis=0),
+        (lax.axis_index("sector") + 1) * ring[0].shape[0],
+        axis=0,
+    )
     norms = []
     psi = wavefunction
     count = lax.axis_size("sector") * psi.size

time: 482 us -> 461 us (0.956)
  local copies, waits for them, and re-layouts: 47.3 us -> 33.1 us
  waiting for transfers between devices: 226 us -> 217 us
    all_gather x1 -> x0, waiting for transfers between devices: 31.1 us -> none  [per_device(): full = lax.all_gather(wavefunction, 'sector', axis=0, tiled=True)]
    ppermute x0 -> x3, waiting for transfers between devices: none -> 22.6 us  [per_device(): lax.ppermute(ring[-1], 'sector', [(dev, (dev + 1) % 4) for dev in range(4)])]
    dynamic_slice x48, local copies, waits for them, and re-layouts: 44 us -> 28.2 us  [apply_tasks(): lax.scan(one_task, start, (left_env, right_env, in_sector, out_sector))]
    unnamed x8 -> x7, waiting for transfers between devices: 56.8 us -> 56.2 us
  transfers between devices with their start and end apart: 6 -> 8, of which waited for: 6 -> 8; matrix products, arithmetic and copies ran while one was open for 0% -> 0% of each run, Pallas kernels for 0% -> 0%
where the time goes in v1:
time: 461 us; the launch traced here: 458 us
  waiting for transfers between devices  217 us (47%)
  loops' own time  94.2 us (20%)
  matrix products  65.1 us (14%)
  local copies, waits for them, and re-layouts  33.1 us (7%)
  blocking collectives  20.9 us (5%)
  between operations  16.7 us (4%)
  other arithmetic  6.63 us (1%)
    psum x2, waiting for transfers between devices, per_device(): sigma = lax.psum(owned, 'term')  115 us
    another operation x2, loops' own time, apply_tasks(): lax.scan(one_task, start, (left_env, right_env, in_sector, out_sector))  94.2 us
    unnamed x7, waiting for transfers between devices  56.2 us
    dot_general x24, matrix products, one_task(): jnp.dot(left, block, precision=lax.Precision.HIGHEST, preferred_element_t...  33 us
    dot_general x24, matrix products, one_task(): jnp.dot(middle, right, precision=lax.Precision.HIGHEST, preferred_element...  32.1 us
    dynamic_slice x48, local copies, waits for them, and re-layouts, apply_tasks(): lax.scan(one_task, start, (left_env, right_env, in_sector, out_sector))  28.2 us
    all_gather x1, waiting for transfers between devices, per_device(): full = lax.all_gather(psi, 'sector', axis=0, tiled=True)  23.8 us
    ppermute x3, waiting for transfers between devices, per_device(): lax.ppermute(ring[-1], 'sector', [(dev, (dev + 1) % 4) for dev in range(4)])  22.6 us
  transfers between devices with their start and end apart: 8, of which 8 were waited for; matrix products, arithmetic and copies ran while one was open for 0% of the time, Pallas kernels for 0%

profile of v1, /device:TPU:0, one launch (start us, length us, event | category | flops | bytes accessed | tf_op | source)
XLA Modules:
  0.0 458.0 jit_solution(14426616952889608220)
XLA Ops:
  7.2 3.0 collective-permute-start
  10.2 7.5 %collective-permute-done = f32[1,256,256]{2,1,0:T(8,128)S(1)} collective-permute-done((f32[1,256,256]{2,1,0:T(8,128)}, f32[1,256,256]{2,1,0:T(8,128)S(1)}, u32[]{:S(2)}, u32[]{:S(2)}) %collective-permute-start) | collective-permute-done | bytes 262176 | tf_op jit(solution)/shard_map/ppermute | solution.py:38
  18.5 7.6 %collective-permute-done.1 = f32[1,256,256]{2,1,0:T(8,128)S(1)} collective-permute-done((f32[1,256,256]{2,1,0:T(8,128)S(1)}, f32[1,256,256]{2,1,0:T(8,128)S(1)}, u32[]{:S(2)}, u32[]{:S(2)}) %collective-permute-start.1) | collective-permute-done | bytes 262176 | tf_op jit(solution)/shard_map/ppermute | solution.py:38
  26.1 7.5 %collective-permute-done.2 = f32[1,256,256]{2,1,0:T(8,128)S(1)} collective-permute-done((f32[1,256,256]{2,1,0:T(8,128)S(1)}, f32[1,256,256]{2,1,0:T(8,128)S(1)}, u32[]{:S(2)}, u32[]{:S(2)}) %collective-permute-start.2) | collective-permute-done | bytes 262176 | tf_op jit(solution)/shard_map/ppermute | solution.py:38
  35.4 93.6 %while.20 = (s32[]{:T(128)}, f32[4,256,256]{2,1,0:T(8,128)S(1)}, s32[12]{0:T(128)S(1)}, f32[12,256,256]{2,1,0:T(8,128)}, s32[12]{0:T(128)S(1)}, /*index=5*/f32[4...) while((s32[]{:T(128)}, f32[4,256,256]{2,1,0:T(8,128)S(1)}, ...), condition=%wide.region_1.2_spmd, body=%wide.region_0.1_spmd.sunk | while | flops 402718720 | bytes 2360525 | solution.py:25
  130.0 28.1 %reduce-scatter.7.cloned.1.call-done = f32[1,256,256]{2,1,0:T(8,128)} async-done(((f32[4,256,256]{2,1,0:T(8,128)}), f32[1,256,256]{2,1,0:T(8,128)}) %reduce-scatter.7.cloned.1.call-update) | async-done | bytes 262160
  158.7 57.1 %all-reduce.6.cloned.1.call-done = f32[1,256,256]{2,1,0:T(8,128)} async-done(((f32[1,256,256]{2,1,0:T(8,128)}), f32[1,256,256]{2,1,0:T(8,128)}) %all-reduce.6.cloned.1.call-update) | async-done | bytes 262160 | tf_op jit(solution)/shard_map/psum | solution.py:50
  215.8 2.4 multiply_reduce_fusion.3
  218.2 10.4 %psum.43 = f32[]{:T(128)} all-reduce(f32[]{:T(128)} %get-tuple-element.111), channel_id=1, replica_groups=mesh['sector'=4,'term'=8] {'sector'}, use_global_device_ids=true, to_apply=%region_5.6 | all-reduce | flops 1 | bytes 8 | tf_op jit(solution)/shard_map/psum | solution.py:52
  230.1 23.8 %all-gather.2.cloned.1.call-done = f32[4,256,256]{2,1,0:T(8,128)} async-done(((f32[1,256,256]{2,1,0:T(8,128)}), f32[4,256,256]{2,1,0:T(8,128)}) %all-gather.2.cloned.1.call-update) | async-done | bytes 1048592 | tf_op jit(solution)/shard_map/all_gather | solution.py:56
  254.1 94.6 %while.21 = (s32[]{:T(128)}, f32[4,256,256]{2,1,0:T(8,128)S(1)}, s32[12]{0:T(128)S(1)}, f32[12,256,256]{2,1,0:T(8,128)}, s32[12]{0:T(128)S(1)}, /*index=5*/f32[4...) while((s32[]{:T(128)}, f32[4,256,256]{2,1,0:T(8,128)S(1)}, ...), condition=%wide.region_7.8_spmd, body=%wide.region_6.7_spmd.sunk | while | flops 402718720 | bytes 2360525 | solution.py:25
  256.6 1.4 fusion.47
  264.5 1.4 fusion.47
  272.4 1.4 fusion.47
  280.2 1.4 fusion.47
  288.1 1.4 fusion.47
  296.0 1.4 fusion.47
  303.9 1.4 fusion.47
  311.8 1.4 fusion.47
  327.5 1.4 fusion.47
  349.7 28.0 %reduce-scatter.9.cloned.1.call-done = f32[1,256,256]{2,1,0:T(8,128)} async-done(((f32[4,256,256]{2,1,0:T(8,128)}), f32[1,256,256]{2,1,0:T(8,128)}) %reduce-scatter.9.cloned.1.call-update) | async-done | bytes 262160
  377.8 57.6 %all-reduce.8.cloned.1.call-done = f32[1,256,256]{2,1,0:T(8,128)} async-done(((f32[1,256,256]{2,1,0:T(8,128)}), f32[1,256,256]{2,1,0:T(8,128)}) %all-reduce.8.cloned.1.call-update) | async-done | bytes 262160 | tf_op jit(solution)/shard_map/psum | solution.py:50
  435.4 2.2 multiply_reduce_fusion.2
  437.6 10.5 %all-reduce.2 = (f32[]{:T(128)}, f32[]{:T(128)}, f32[]{:T(128)}) all-reduce(f32[]{:T(128)} %get-tuple-element.109, f32[]{:T(128)} %get-tuple-element.114, f32[]{:T(128)} %get-tuple-element.113), channel_id=1, replica_groups=mesh['sector'=4,'term'=8] {'sector'}, use_global_device_ids=true, to_apply=%region_11.12 | all-reduce | flops 3 | bytes 24 | tf_op jit(solution)/shard_map/psum | solution.py:52
  (152 shorter events, 88.6 us)
Async XLA Ops:
  7.2 27.6 %copy-start.2 = (f32[1,256,256]{2,1,0:T(8,128)S(1)}, f32[1,256,256]{2,1,0:T(8,128)}, u32[]{:S(2)}) copy-start(f32[1,256,256]{2,1,0:T(8,128)} %param.11) | copy-start | bytes 786436
  7.2 150.9 %reduce-scatter.7.cloned.1.call-start = ((), (), s32[]{:S(2)}) async-start(), calls=%async_computation.5 | async-start | bytes 1310720
  7.2 10.5 %collective-permute-start = (f32[1,256,256]{2,1,0:T(8,128)}, f32[1,256,256]{2,1,0:T(8,128)S(1)}, u32[]{:S(2)}, u32[]{:S(2)}) collective-permute-start(f32[1,256,256]{2,1,0:T(8,128)} %param.11), channel_id=1, source_target_pairs={{0,8},{8,16},{16,24},{24,0},{1,9},{9,17},{17,25},{25,1},{2,10},{10... | collective-permute-start | bytes 786440 | tf_op jit(solution)/shard_map/ppermute | solution.py:38
  17.7 8.4 %collective-permute-start.1 = (f32[1,256,256]{2,1,0:T(8,128)S(1)}, f32[1,256,256]{2,1,0:T(8,128)S(1)}, u32[]{:S(2)}, u32[]{:S(2)}) collective-permute-start(f32[1,256,256]{2,1,0:T(8,128)S(1)} %collective-permute-done), channel_id=1, source_target_pairs={{0,8},{8,16},{16,24},{24,0},{1,9},{9,17},{17,25},{25,1},{2,10},{10... | collective-permute-start | bytes 786440 | tf_op jit(solution)/shard_map/ppermute | solution.py:38
  26.1 7.5 %collective-permute-start.2 = (f32[1,256,256]{2,1,0:T(8,128)S(1)}, f32[1,256,256]{2,1,0:T(8,128)S(1)}, u32[]{:S(2)}, u32[]{:S(2)}) collective-permute-start(f32[1,256,256]{2,1,0:T(8,128)S(1)} %collective-permute-done.1), channel_id=1, source_target_pairs={{0,8},{8,16},{16,24},{24,0},{1,9},{9,17},{17,25},{25,1},{2,10},{10... | collective-permute-start | bytes 786440 | tf_op jit(solution)/shard_map/ppermute | solution.py:38
  34.7 0.7 copy-start.5
  34.7 0.7 copy-start.6
  35.4 122.8 %copy-start.4 = (f32[2]{0:T(128)S(1)}, f32[2]{0:T(128)}, u32[]{:S(2)}) copy-start(f32[2]{0:T(128)} %param.17) | copy-start | bytes 28
  35.4 180.5 %copy-start.3 = (f32[1,256,256]{2,1,0:T(8,128)S(1)}, f32[1,256,256]{2,1,0:T(8,128)}, u32[]{:S(2)}) copy-start(f32[1,256,256]{2,1,0:T(8,128)} %param.16) | copy-start | bytes 786436
  128.9 1.0 copy-start.1
  129.9 85.9 %all-reduce.6.cloned.1.call-start = ((), (), s32[]{:S(2)}) async-start(), calls=%async_computation.2 | async-start | bytes 524288 | tf_op jit(solution)/shard_map/psum | solution.py:50
  158.1 95.9 %all-gather.2.cloned.1.call-start = ((), (), s32[]{:S(2)}) async-start(), calls=%async_computation.3 | async-start | bytes 1310720 | tf_op jit(solution)/shard_map/all_gather | solution.py:56
  230.1 147.6 %reduce-scatter.9.cloned.1.call-start = ((), (), s32[]{:S(2)}) async-start(), calls=%async_computation.6 | async-start | bytes 1310720
  348.7 1.0 copy-start
  349.7 85.7 %all-reduce.8.cloned.1.call-start = ((), (), s32[]{:S(2)}) async-start(), calls=%async_computation.4 | async-start | bytes 524288 | tf_op jit(solution)/shard_map/psum | solution.py:50
Sparse Core Ops, SparseCore 0:
  130.1 27.9 reduce-scatter.6
  160.4 55.4 all-reduce.5
  230.2 23.7 all-gather.1
  349.8 27.9 reduce-scatter.8
  379.9 55.4 all-reduce.7
